TPU v7x, 512 devices: a whole 4x4x16 slice. The times are simulated.
512 devices in a mesh: dom: 64 (over y, z_lo, core), cls: 8 (over z_hi, x).
Axes of the slice: x: 4, y: 4, z: 16 (z_hi: 2, z_lo: 8; z = z_hi * 8 + z_lo), core: 2. Of those that a mesh axis runs over, the one named last changes fastest.
Arguments:
- particles: bfloat16 [36864, 4096], P('dom'), may hold values from -6 to 6
- shift_index: int32 [36864], P('dom'), may hold values from 0 to 24
- prev_class: int32 [36864], P('dom'), may hold values from 0 to 63
- prev_rotation: int32 [36864], P('dom'), may hold values from 0 to 23
- precision: float32 [36864], P('dom'), may hold values from 0.25 to 300
- references: bfloat16 [64, 98304], P('cls', 'dom')
Outputs:
- new_references: float32 [64, 98304], P('cls', 'dom')
- log_evidence: float32 [36864], P('dom')
All inputs are finite; a program needn't handle non-finite values.
Results may differ from a plain program's by a relative error of at most 0.0039.
Values may be sent and summed in bfloat16 or wider, within the bound.
No kernel may reach another device: no remote copies, remote signals or barrier semaphores. Data moves between devices by JAX's collectives and lax.ppermute only.
A program may use at most 64 MiB of HBM per device.

v0:
```python
import math
import jax
import jax.numpy as jnp
from jax import lax
from jax.sharding import PartitionSpec as P

BOX = 64
F = 4096
R = 24
two_pi = 2.0 * math.pi
shift_side = 5
class_reward = 1.0
prior_mass = 1.0


def shift_particles(particles, shift_index, box_side):
    half_width = particles.shape[1] // 2
    frequency = jnp.arange(half_width, dtype=jnp.int32)
    freq_x = frequency % box_side - box_side // 2
    freq_y = frequency // box_side
    step_x = shift_index % shift_side - 2
    step_y = shift_index // shift_side - 2
    phase_int = (freq_x[None, :] * step_x[:, None] + freq_y[None, :] * step_y[:, None]) % box_side
    phase_angle = phase_int.astype(jnp.float32) * (two_pi / box_side)
    cosine_values = jnp.cos(phase_angle)
    sine_values = jnp.sin(phase_angle)
    real_part = particles[:, :half_width].astype(jnp.float32)
    imag_part = particles[:, half_width:].astype(jnp.float32)
    out_real = real_part * cosine_values + imag_part * sine_values
    out_imag = imag_part * cosine_values - real_part * sine_values
    return jnp.concatenate([out_real, out_imag], axis=1).astype(jnp.bfloat16)


def prior_term(prev_class, prev_rotation, class_ids, rotation_ids, rotations):
    rotation_distance = jnp.abs(rotation_ids[None, :] - prev_rotation[:, None])
    rotation_distance = jnp.minimum(rotation_distance, rotations - rotation_distance).astype(
        jnp.float32
    )
    prior_spread_width = rotations / 8.0
    match_flags = (class_ids[None, :] == prev_class[:, None]).astype(jnp.float32)
    return (
        -rotation_distance * rotation_distance / (2.0 * prior_spread_width * prior_spread_width)
        + class_reward * match_flags
    )


def on_device(particles, shift_index, prev_class, prev_rotation, precision, references):
    local_classes = references.shape[0]
    columns = references.shape[1]
    gathered = lax.all_gather(references, "dom", axis=1, tiled=True)
    table = gathered.reshape(local_classes * R, F)
    half_norm = 0.5 * jnp.sum(jnp.square(table.astype(jnp.float32)), axis=1)
    candidate = jnp.arange(local_classes * R, dtype=jnp.int32)
    class_ids = lax.axis_index("cls") * local_classes + candidate // R
    rotation_ids = candidate % R
    shifted = shift_particles(particles, shift_index, BOX)
    correlation = lax.dot_general(
        shifted, table, (((1,), (1,)), ((), ())), preferred_element_type=jnp.float32
    )
    scores = precision[:, None] * (correlation - half_norm[None, :])
    scores = scores + prior_term(prev_class, prev_rotation, class_ids, rotation_ids, R)
    local_top = jnp.max(scores, axis=1)
    top_score = lax.pmax(local_top, "cls")
    exponent = jnp.exp(scores - top_score[:, None])
    total_mass = lax.psum(jnp.sum(exponent, axis=1), "cls")
    probs = exponent / total_mass[:, None]
    weights = probs.astype(jnp.bfloat16)
    numerator = lax.dot_general(
        weights, shifted, (((0,), (0,)), ((), ())), preferred_element_type=jnp.float32
    )
    numerator = numerator.reshape(local_classes, R * F)
    occupancy = jnp.sum(probs, axis=0).reshape(local_classes, R)
    start = lax.axis_index("dom") * columns
    summed, occupancy = lax.psum((numerator, occupancy), "dom")
    mine = lax.dynamic_slice_in_dim(summed, start, columns, 1)
    spread = jnp.broadcast_to(occupancy[:, :, None], (local_classes, R, F)).reshape(
        local_classes, R * F
    )
    mass_columns = lax.dynamic_slice_in_dim(spread, start, columns, 1)
    refreshed_references = mine / (mass_columns + prior_mass)
    evidence = top_score + jnp.log(total_mass)
    return (refreshed_references, evidence)


def solution(mesh):
    return jax.shard_map(
        on_device,
        mesh=mesh,
        in_specs=(P("dom", None), P("dom"), P("dom"), P("dom"), P("dom"), P("cls", "dom")),
        out_specs=(P("cls", "dom"), P("dom")),
        check_vma=False,
    )
```

profile of v0, /device:TPU:1, one launch (start us, length us, event | category | flops | bytes accessed | tf_op | source)
XLA Modules:
  0.0 1063.9 jit_solution(16293794462568525287)
XLA Ops:
  7.2 0.0 all-gather.2.cloned.1.call-start
  7.2 0.7 all-gather.2.cloned.1.call-update
  7.9 0.0 all-reduce.2.cloned.1.call-start
  8.0 0.7 fusion.28
  8.7 23.3 %fusion.1 = (bf16[576,2048]{1,0:T(8,128)(2,1)}, bf16[576,2048]{1,0:T(8,128)(2,1)}) fusion(s32[576]{0:T(1024)S(1)} %get-tuple-element.5, s32[2048]{0:T(1024)S(1)} %get-tuple-element.8, s32[576]{0:T(1024)S(1)} %get-tuple-element.4, s32[2048]{0:T(1024)S(1)} %get-tuple-element.9, bf16[576,4096]{1,0:T(8,128)(2,1)} %param.6), kind=kLoop, calls=%fused_computation.8 | loop fusion | flops 30670848 | bytes 9458176 | tf_op jit(solution)/shard_map/convert
  32.0 104.3 %all-gather.2.cloned.1.call-done = bf16[8,98304]{1,0:T(8,128)(2,1)} async-done(((bf16[8,1536]{1,0:T(8,128)(2,1)}), bf16[8,98304]{1,0:T(8,128)(2,1)}) %all-gather.2.cloned.1.call-update) | async-done | bytes 1572880 | tf_op jit(solution)/shard_map/all_gather | solution.py:50
  136.3 2.1 reshape.71
  138.4 0.4 multiply_reduce_fusion
  138.8 0.0 copy-done.2
  138.8 4.3 fusion.35
  143.1 38.3 %pmax.7 = f32[576]{0:T(1024)S(1)} all-reduce(f32[576]{0:T(1024)S(1)} %get-tuple-element.6), channel_id=1, replica_groups=mesh['dom'=64,'cls'=8] {'cls'}, use_global_device_ids=true, to_apply=%region_2.3 | all-reduce | flops 576 | bytes 4608 | tf_op jit(solution)/shard_map/pmax | solution.py:63
  181.5 0.1 fusion.18
  181.6 29.9 %psum.21 = f32[576]{0:T(1024)S(1)} all-reduce(f32[576]{0:T(1024)S(1)} %fusion.18), channel_id=1, replica_groups=mesh['dom'=64,'cls'=8] {'cls'}, use_global_device_ids=true, to_apply=%region_4.5 | all-reduce | flops 576 | bytes 4608 | tf_op jit(solution)/shard_map/psum | solution.py:65
  211.5 3.9 fusion.7
  215.5 2.3 reshape.72
  217.7 0.0 all-reduce.2.cloned.1.call-update
  217.7 1.2 fusion.20
  218.9 0.1 reshape.73
  219.0 217.7 %psum.23 = f32[8,24]{1,0:T(8,128)S(1)} all-reduce(f32[8,24]{1,0:T(8,128)S(1)} %reshape.73), channel_id=1, replica_groups=mesh['dom'=64,'cls'=8] {'dom'}, use_global_device_ids=true, to_apply=%region_7.8 | all-reduce | flops 192 | bytes 1536 | tf_op jit(solution)/shard_map/psum | solution.py:74
  436.7 0.1 copy.8
  436.8 0.6 log_add_fusion
  437.4 618.0 %all-reduce.2.cloned.1.call-done = f32[8,98304]{1,0:T(8,128)} async-done(((f32[8,98304]{1,0:T(8,128)}), f32[8,98304]{1,0:T(8,128)}) %all-reduce.2.cloned.1.call-update) | async-done | bytes 3145744 | tf_op jit(solution)/shard_map/psum | solution.py:74
  1055.3 0.3 broadcast_in_dim.2
  1055.6 1.4 add_divide_fusion
  (10 shorter events, 0.0 us)
Async XLA Ops:
  7.2 129.1 %all-gather.2.cloned.1.call-start = ((), (), s32[]{:S(2)}) async-start(), calls=%async_computation | async-start | bytes 1597440 | tf_op jit(solution)/shard_map/all_gather | solution.py:50
  7.9 1047.4 %all-reduce.2.cloned.1.call-start = ((), (), s32[]{:S(2)}) async-start(), calls=%async_computation.1 | async-start | bytes 6291456 | tf_op jit(solution)/shard_map/psum | solution.py:74
  32.0 106.8 %copy-start.1 = (s32[576]{0:T(1024)S(1)}, s32[576]{0:T(1024)}, u32[]{:S(2)}) copy-start(s32[576]{0:T(1024)} %param.8) | copy-start | bytes 6916
  32.0 106.8 %copy-start.2 = (s32[576]{0:T(1024)S(1)}, s32[576]{0:T(1024)}, u32[]{:S(2)}) copy-start(s32[576]{0:T(1024)} %param.9) | copy-start | bytes 6916
  32.0 106.8 %copy-start.3 = (f32[576]{0:T(1024)S(1)}, f32[576]{0:T(1024)}, u32[]{:S(2)}) copy-start(f32[576]{0:T(1024)} %param.10) | copy-start | bytes 6916
  143.1 38.4 %copy-start = (f32[576,192]{0,1:T(8,128)}, f32[576,192]{0,1:T(8,128)S(1)}, u32[]{:S(2)}) copy-start(f32[576,192]{0,1:T(8,128)S(1)} %get-tuple-element.7) | copy-start | bytes 1327108
Sparse Core Ops, SparseCore 0:
  10.1 126.0 all-gather.1
  217.9 837.4 all-reduce.1
where the time goes:
time: 1060 us
  waiting for transfers between devices  723 us (68%)
  blocking collectives  286 us (27%)
  other arithmetic  27.7 us (3%)
  between operations  14.1 us (1%)
    psum x1, waiting for transfers between devices, on_device(): summed, occupancy = lax.psum((numerator, occupancy), 'dom')  618 us
    psum x1, blocking collectives, on_device(): summed, occupancy = lax.psum((numerator, occupancy), 'dom')  218 us
    all_gather x1, waiting for transfers between devices, on_device(): gathered = lax.all_gather(references, 'dom', axis=1, tiled=True)  104 us
    pmax x1, blocking collectives, on_device(): top_score = lax.pmax(local_top, 'cls')  38.3 us
    psum x1, blocking collectives, on_device(): total_mass = lax.psum(jnp.sum(exponent, axis=1), 'cls')  29.9 us
    another operation x1, other arithmetic  23.3 us
  transfers between devices with their start and end apart: 2, of which 2 were waited for; matrix products, arithmetic and copies ran while one was open for 2% of the time, Pallas kernels for 0%

commit v1 on v0

--- a/solution.py
+++ b/solution.py
@@ -47,7 +47,9 @@
 def on_device(particles, shift_index, prev_class, prev_rotation, precision, references):
     local_classes = references.shape[0]
     columns = references.shape[1]
-    gathered = lax.all_gather(references, "dom", axis=1, tiled=True)
+    gathered = jnp.concatenate(
+        lax.all_to_all(jnp.stack([references] * lax.axis_size("dom")), "dom", 0, 0), axis=1
+    )
     table = gathered.reshape(local_classes * R, F)
     half_norm = 0.5 * jnp.sum(jnp.square(table.astype(jnp.float32)), axis=1)
     candidate = jnp.arange(local_classes * R, dtype=jnp.int32)

time: 1060 us -> 1030 us (0.972)
  waiting for transfers between devices: 723 us -> 670 us
  starting transfers between devices: 0.08 us -> 17.3 us
    all_gather x1 -> x0, waiting for transfers between devices: 104 us -> none  [on_device(): gathered = lax.all_gather(references, 'dom', axis=1, tiled=True)]
    all_to_all x0 -> x1, waiting for transfers between devices: none -> 50.1 us  [on_device(): lax.all_to_all(jnp.stack([references] * lax.axis_size('dom')), 'dom', 0, 0)]
    all_to_all x0 -> x1, starting transfers between devices: none -> 17.2 us  [on_device(): lax.all_to_all(jnp.stack([references] * lax.axis_size('dom')), 'dom', 0, 0)]
where the time goes in v1:
time: 1030 us
  waiting for transfers between devices  670 us (65%)
  blocking collectives  285 us (28%)
  other arithmetic  27.1 us (3%)
  starting transfers between devices  17.3 us (2%)
  between operations  14.2 us (1%)
    psum x1, waiting for transfers between devices, on_device(): summed, occupancy = lax.psum((numerator, occupancy), 'dom')  620 us
    psum x1, blocking collectives, on_device(): summed, occupancy = lax.psum((numerator, occupancy), 'dom')  217 us
    all_to_all x1, waiting for transfers between devices, on_device(): lax.all_to_all(jnp.stack([references] * lax.axis_size('dom')), 'dom', 0, 0)  50.1 us
    pmax x1, blocking collectives, on_device(): top_score = lax.pmax(local_top, 'cls')  38.1 us
    psum x1, blocking collectives, on_device(): total_mass = lax.psum(jnp.sum(exponent, axis=1), 'cls')  29.9 us
    another operation x1, other arithmetic  23.3 us
  transfers between devices with their start and end apart: 2, of which 2 were waited for; matrix products, arithmetic and copies ran while one was open for 2% of the time, Pallas kernels for 0%

profile of v1, /device:TPU:1, one launch (start us, length us, event | category | flops | bytes accessed | tf_op | source)
XLA Modules:
  0.0 1029.1 jit_solution(6891757854963655140)
XLA Ops:
  7.2 2.0 stack.2
  9.2 17.2 %all-to-all-start = ((bf16[64,8,1536]{2,1,0:T(8,128)(2,1)}), bf16[64,8,1536]{2,1,0:T(8,128)(2,1)S(1)}, u32[]{:S(2)}, u32[]{:S(2)}) async-start(bf16[64,8,1536]{2,1,0:T(8,128)(2,1)} %stack.2), calls=%async_computation | async-start | bytes 3145728 | tf_op jit(solution)/shard_map/all_to_all | solution.py:51
  26.4 0.0 all-reduce.2.cloned.1.call-start
  26.5 0.0 copy-done.1
  26.5 23.3 %fusion.1 = (bf16[576,2048]{1,0:T(8,128)(2,1)}, bf16[576,2048]{1,0:T(8,128)(2,1)}) fusion(s32[576]{0:T(1024)S(1)} %get-tuple-element.5, s32[2048]{0:T(1024)S(1)} %get-tuple-element.8, s32[576]{0:T(1024)S(1)} %get-tuple-element.4, s32[2048]{0:T(1024)S(1)} %get-tuple-element.9, bf16[576,4096]{1,0:T(8,128)(2,1)} %param.6), kind=kLoop, calls=%fused_computation.8 | loop fusion | flops 30670848 | bytes 9458176 | tf_op jit(solution)/shard_map/convert
  49.8 50.1 %all-to-all-done = bf16[64,8,1536]{2,1,0:T(8,128)(2,1)S(1)} async-done(((bf16[64,8,1536]{2,1,0:T(8,128)(2,1)}), bf16[64,8,1536]{2,1,0:T(8,128)(2,1)S(1)}, u32[]{:S(2)}, u32[]{:S(2)}) %all-to-all-start) | async-done | bytes 1572896 | tf_op jit(solution)/shard_map/all_to_all | solution.py:51
  99.9 0.5 copy.9
  100.4 1.9 reshape_reshape.3
  102.3 0.4 multiply_reduce_fusion
  102.7 4.3 fusion.35
  107.0 38.1 %pmax.7 = f32[576]{0:T(1024)S(1)} all-reduce(f32[576]{0:T(1024)S(1)} %get-tuple-element.6), channel_id=1, replica_groups=mesh['dom'=64,'cls'=8] {'cls'}, use_global_device_ids=true, to_apply=%region_2.3 | all-reduce | flops 576 | bytes 4608 | tf_op jit(solution)/shard_map/pmax | solution.py:65
  145.2 0.1 fusion.18
  145.3 29.9 %psum.21 = f32[576]{0:T(1024)S(1)} all-reduce(f32[576]{0:T(1024)S(1)} %fusion.18), channel_id=1, replica_groups=mesh['dom'=64,'cls'=8] {'cls'}, use_global_device_ids=true, to_apply=%region_4.5 | all-reduce | flops 576 | bytes 4608 | tf_op jit(solution)/shard_map/psum | solution.py:67
  175.2 3.9 fusion.7
  179.1 2.3 reshape.74
  181.4 0.0 all-reduce.2.cloned.1.call-update
  181.4 1.2 fusion.20
  182.6 0.1 reshape.75
  182.7 216.9 %psum.23 = f32[8,24]{1,0:T(8,128)S(1)} all-reduce(f32[8,24]{1,0:T(8,128)S(1)} %reshape.75), channel_id=1, replica_groups=mesh['dom'=64,'cls'=8] {'dom'}, use_global_device_ids=true, to_apply=%region_7.8 | all-reduce | flops 192 | bytes 1536 | tf_op jit(solution)/shard_map/psum | solution.py:76
  399.6 0.1 copy.10
  399.6 0.6 log_add_fusion
  400.2 620.2 %all-reduce.2.cloned.1.call-done = f32[8,98304]{1,0:T(8,128)} async-done(((f32[8,98304]{1,0:T(8,128)}), f32[8,98304]{1,0:T(8,128)}) %all-reduce.2.cloned.1.call-update) | async-done | bytes 3145744 | tf_op jit(solution)/shard_map/psum | solution.py:76
  1020.5 0.3 broadcast_in_dim.2
  1020.8 1.4 add_divide_fusion
  (13 shorter events, 0.1 us)
Async XLA Ops:
  7.2 19.3 %copy-start.1 = (s32[576]{0:T(1024)S(1)}, s32[576]{0:T(1024)}, u32[]{:S(2)}) copy-start(s32[576]{0:T(1024)} %param.7) | copy-start | bytes 6916
  9.2 90.7 %all-to-all-start = ((bf16[64,8,1536]{2,1,0:T(8,128)(2,1)}), bf16[64,8,1536]{2,1,0:T(8,128)(2,1)S(1)}, u32[]{:S(2)}, u32[]{:S(2)}) async-start(bf16[64,8,1536]{2,1,0:T(8,128)(2,1)} %stack.2), calls=%async_computation | async-start | bytes 3145728 | tf_op jit(solution)/shard_map/all_to_all | solution.py:51
  26.4 994.1 %all-reduce.2.cloned.1.call-start = ((), (), s32[]{:S(2)}) async-start(), calls=%async_computation.1 | async-start | bytes 6291456 | tf_op jit(solution)/shard_map/psum | solution.py:76
  49.8 52.9 %copy-start.2 = (s32[576]{0:T(1024)S(1)}, s32[576]{0:T(1024)}, u32[]{:S(2)}) copy-start(s32[576]{0:T(1024)} %param.8) | copy-start | bytes 6916
  49.8 52.9 %copy-start.3 = (s32[576]{0:T(1024)S(1)}, s32[576]{0:T(1024)}, u32[]{:S(2)}) copy-start(s32[576]{0:T(1024)} %param.9) | copy-start | bytes 6916
  49.8 52.9 %copy-start.4 = (f32[576]{0:T(1024)S(1)}, f32[576]{0:T(1024)}, u32[]{:S(2)}) copy-start(f32[576]{0:T(1024)} %param.10) | copy-start | bytes 6916
  107.0 38.2 %copy-start = (f32[576,192]{0,1:T(8,128)}, f32[576,192]{0,1:T(8,128)S(1)}, u32[]{:S(2)}) copy-start(f32[576,192]{0,1:T(8,128)S(1)} %get-tuple-element.7) | copy-start | bytes 1327108
Sparse Core Ops, SparseCore 0:
  181.5 838.9 all-reduce.1
